TPU v7x, 512 devices: a whole 4x8x8 slice. The times are simulated.
512 devices in a mesh: region: 256 (over z, y, x), dom: 2 (over core).
Axes of the slice: x: 4, y: 8, z: 8, core: 2. Of those that a mesh axis runs over, the one named last changes fastest.
Arguments:
- fine_state: float32 [262144, 128], P(('region', 'dom')), may hold values from -6 to 6
- fine_nbr: int32 [16, 262144], P(None, ('region', 'dom')), may hold values from 0 to 575
- fine_mask: int32 [16, 262144], P(None, ('region', 'dom')), may hold values 0 or 1
- send_rows: int32 [4, 8192], P(None, ('region', 'dom')), may hold values from 0 to 511
- coarse_nbr: int32 [16, 65536], P(None, ('region', 'dom')), may hold values from 0 to 255
- coarse_mask: int32 [16, 65536], P(None, ('region', 'dom')), may hold values 0 or 1
- parent: int32 [262144], P(('region', 'dom')), may hold values from 0 to 65535, as said below
- interp_share: int32 [262144], P(('region', 'dom')), may hold values from 1 to 4
- edge_w: float32 [4, 3, 128, 128], replicated, may hold values from -0.375 to 0.375
- node_w: float32 [4, 3, 128, 128], replicated, may hold values from -0.375 to 0.375
- biases: float32 [4, 4, 128], replicated, may hold values from -3 to 3
Outputs:
- fine_out: float32 [262144, 128], P(('region', 'dom'))
- coarse_out: float32 [65536, 128], P(('region', 'dom'))
Inputs may be any that keep to these rules, and one draw needn't show every extreme that they name: `parent`: of the 512 fine nodes of block (r, d), 448 have parents in coarse blocks of region r, at most 384 in any one block and exactly 384 in some block; 32 have parents in blocks of region r-1 and 32 in blocks of region r+1 (periodic), at most 32 in any one block and exactly 32 in some block of each.
All inputs are finite; a program needn't handle non-finite values. No bound on the sum of `fine_mask` or of `coarse_mask` on one device may be relied on, other than what follows from the above.
Results may differ from a plain program's by a relative error of at most 0.0001.
Values sent between devices are 32-bit elements; how exact they have to be, the bound alone decides.
A program may use at most 64 MiB of HBM per device.

v0:
```python
import functools

import jax
import jax.numpy as jnp
from jax import lax
from jax.experimental import pallas as pl
from jax.experimental.pallas import tpu as pltpu
from jax.sharding import PartitionSpec as P

MESH = pl.DeviceIdType.MESH
EPS = 1e-05
F32 = jnp.float32
BF16 = jnp.bfloat16
W = 128
SLOTS = 16
F = 512
H = 16
C = 128
SIDE = 32


def halves(x):
    hi = x.astype(BF16)
    lo = (x - hi.astype(F32)).astype(BF16)
    return hi, lo


def split(x):
    return jnp.concatenate(halves(x), axis=0)


def dot(a, b):
    return lax.dot_general(a, b, (((1,), (0,)), ((), ())), preferred_element_type=F32)


def dot_nt(a, b):
    return lax.dot_general(a, b, (((1,), (1,)), ((), ())), preferred_element_type=F32)


def fold(y):
    return y[:W] + y[W:]


def fold_lanes(y):
    return y[:, :W] + y[:, W:]


def one_hot(index_row, depth):
    n = index_row.shape[1]
    blocks = []
    for base in range(0, depth, 256):
        size = min(256, depth - base)
        rows = lax.broadcasted_iota(jnp.int32, (size, n), 0)
        blocks.append((rows == (index_row - base)).astype(F32).astype(BF16))
    return blocks[0] if len(blocks) == 1 else jnp.concatenate(blocks, axis=0)


def stacked(w, centred=False):
    t = w.T
    if centred:
        t = t - jnp.sum(t, axis=0, keepdims=True) * (1.0 / W)
    s = split(t)
    return jnp.concatenate([s, s], axis=1)


def scale_of(centred):
    return lax.rsqrt(jnp.sum(centred * centred, axis=0, keepdims=True) * (1.0 / W) + EPS)


def centred_bias(column):
    return column - jnp.sum(column, axis=0, keepdims=True) * (1.0 / W)


def message(gathered, own, second, second_bias, valid_row):
    hidden = jnp.maximum(fold(gathered) + own, 0.0)
    centred = fold(dot(second, split(hidden))) + second_bias
    return centred * (scale_of(centred) * valid_row)


def node_update(rows, own_part, total, node1, node2, bias3):
    inner = jnp.maximum(own_part + fold(dot(node1, split(total))), 0.0)
    centred = fold(dot(node2, split(inner))) + bias3
    return rows + centred * scale_of(centred)


def kernel(
    regions,
    x_ref,
    nbr_ref,
    mask_ref,
    send_ref,
    cnbr_ref,
    cmask_ref,
    parent_ref,
    share_ref,
    edge_ref,
    node_ref,
    bias_ref,
    out_ref,
    cout_ref,
    tile_ref,
    wts,
    src_proj,
    own_ref,
    node_own,
    total_ref,
    fine_ref,
    rim_pick,
    side_pick,
    own_hot,
    rim_send,
    rim_recv,
    meta_send,
    meta_recv,
    tot_send,
    tot_recv,
    part_send,
    part_recv,
    side_send,
    side_recv,
    mid_send,
    mid_recv,
    co_send,
    co_recv,
    reply_send,
    reply_recv,
    rim2_send,
    rim2_recv,
    send_sem,
    recv_sem,
):
    r = lax.axis_index("region")
    d = lax.axis_index("dom")
    up = lax.rem(r + 1, regions)
    down = lax.rem(r + regions - 1, regions)
    other = 1 - d
    peers = [(down, 0), (down, 1), (up, 0), (up, 1), (r, other)]
    barrier = pltpu.get_barrier_semaphore()
    for peer in peers:
        pl.semaphore_signal(barrier, inc=1, device_id=peer, device_id_type=MESH)

    def copy(k, src, dst, peer):
        return pltpu.make_async_remote_copy(
            src_ref=src,
            dst_ref=dst,
            send_sem=send_sem.at[k],
            recv_sem=recv_sem.at[k],
            device_id=peer,
            device_id_type=MESH,
        )

    def rim_copies(base, src, dst):
        return [
            copy(base, src.at[pl.ds(0, H)], dst.at[pl.ds(0, H)], (up, d)),
            copy(base + 1, src.at[pl.ds(H, H)], dst.at[pl.ds(H, H)], (down, d)),
            copy(base + 2, src.at[pl.ds(2 * H, 2 * H)], dst.at[pl.ds(2 * H, 2 * H)], (r, other)),
        ]

    def side_copies(base, src, dst):
        copies = []
        for way, region in ((0, down), (1, up)):
            for e in range(2):
                copies.append((way, e, region))
        return [
            pltpu.make_async_remote_copy(
                src_ref=src[way][e],
                dst_ref=dst.at[2 * (1 - way) + d],
                send_sem=send_sem.at[base + 2 * way + e],
                recv_sem=recv_sem.at[base + 2 * (1 - way) + d],
                device_id=(region, e),
                device_id_type=MESH,
            )
            for way, e, region in copies
        ]

    def side_arrivals(base, src, dst):
        return [copy(base + k, src, dst.at[k], (r, other)) for k in range(4)]

    tile_ref[...] = jnp.zeros_like(tile_ref)
    tile_ref[0:4, 0:H] = send_ref[...].astype(F32)
    lists = tile_ref[...].T
    lane = lax.broadcasted_iota(jnp.int32, (H, F), 1)
    picks = []
    for j in range(4):
        column = lists[0:H, j : j + 1].astype(jnp.int32)
        picks.append((lane == column).astype(F32).astype(BF16))
    rim_pick[...] = jnp.concatenate(picks, axis=0)

    x = x_ref[...]
    x_hi, x_lo = halves(x)
    rim_send[...] = dot(rim_pick[...], x_hi) + dot(rim_pick[...], x_lo)

    pl.semaphore_wait(barrier, 5)
    rims = rim_copies(0, rim_send, rim_recv)
    for c in rims:
        c.start()

    parent = parent_ref[...].reshape(1, F)
    share = share_ref[...].reshape(1, F).astype(F32)
    p_region = lax.shift_right_logical(parent, 8)
    p_local = parent & 255
    at_low = p_region == down
    at_high = p_region == up
    here = p_region == r
    own_hot[...] = one_hot(jnp.where(here, (p_local + C * d) & 255, -1), 2 * C)
    flags = jnp.concatenate(
        [at_low.astype(F32), at_high.astype(F32), jnp.zeros((14, F), F32)], axis=0
    ).astype(BF16)
    before = lax.broadcasted_iota(jnp.int32, (F, F), 0) <= lax.broadcasted_iota(
        jnp.int32, (F, F), 1
    )
    ranks = dot(flags, before.astype(F32).astype(BF16)).astype(jnp.int32) - 1
    side_pick[...] = jnp.concatenate(
        [
            one_hot(jnp.where(at_low, ranks[0:1], -1), SIDE),
            one_hot(jnp.where(at_high, ranks[1:2], -1), SIDE),
        ],
        axis=0,
    )
    sub = lax.broadcasted_iota(jnp.int32, (W, F), 0)
    facts = jnp.where(sub < 64, p_local.astype(F32), share).astype(BF16)
    meta_send[...] = dot_nt(side_pick[...], facts)
    low_meta = meta_send.at[pl.ds(0, SIDE)]
    high_meta = meta_send.at[pl.ds(SIDE, SIDE)]
    metas = side_copies(3, ((low_meta, low_meta), (high_meta, high_meta)), meta_recv)
    for c in metas:
        c.start()
    shares16 = jnp.broadcast_to(share, (16, F)).astype(BF16)
    own_total = dot_nt(shares16, own_hot[...])[0:8]
    tot_send[:, 0:C] = own_total[:, C:]
    tot_send[:, C:] = own_total[:, 0:C]
    tot_copy = copy(7, tot_send, tot_recv, (r, other))
    tot_copy.start()

    tile_ref[0:16, :] = bias_ref[...].reshape(16, W)
    biases = tile_ref[...].T

    def bias(layer, k, centre=False):
        column = biases[:, 4 * layer + k : 4 * layer + k + 1]
        return centred_bias(column) if centre else column

    def prepare(layer):
        for k in range(3):
            wts[6 * layer + k] = stacked(edge_ref[layer, k], centred=k == 2)
            wts[6 * layer + 3 + k] = stacked(node_ref[layer, k], centred=k == 2)

    def fine_layer(layer, rows, rows_split, rim_arrivals, rim_rows):
        own_ref[...] = fold(dot(wts[6 * layer], rows_split)) + bias(layer, 0)
        node_own[...] = fold(dot(wts[6 * layer + 3], rows_split)) + bias(layer, 2)
        src_proj[:, 0:F] = split(fold(dot(wts[6 * layer + 1], rows_split)))
        for c in rim_arrivals:
            c.wait_recv()
        rim = jnp.concatenate(halves(rim_rows[...]), axis=1)
        src_proj[:, F:] = split(fold(dot_nt(wts[6 * layer + 1], rim)))
        total_ref[...] = jnp.zeros_like(total_ref)
        bias1 = jnp.broadcast_to(bias(layer, 1, True), (W, F))

        def slot(s, carry):
            hot = one_hot(nbr_ref[pl.ds(s, 1), :], F + 4 * H)
            gathered = dot(src_proj[...], hot)
            valid = mask_ref[pl.ds(s, 1), :].astype(F32)
            total_ref[...] += message(gathered, own_ref[...], wts[6 * layer + 2], bias1, valid)
            return carry

        lax.fori_loop(0, SLOTS, slot, 0)
        return node_update(
            rows,
            node_own[...],
            total_ref[...],
            wts[6 * layer + 4],
            wts[6 * layer + 5],
            bias(layer, 3, True),
        )

    def coarse_layer(layer, rows, own_split, sources):
        own = fold(dot(wts[6 * layer], own_split)) + bias(layer, 0)
        node_part = fold(dot(wts[6 * layer + 3], own_split)) + bias(layer, 2)
        proj = split(fold(dot(wts[6 * layer + 1], sources())))
        own4 = jnp.concatenate([own] * 4, axis=1)
        bias1 = jnp.broadcast_to(bias(layer, 1, True), (W, 4 * C))
        total = jnp.zeros((W, 4 * C), F32)
        for g in range(4):
            ids = jnp.concatenate([cnbr_ref[4 * g + k : 4 * g + k + 1, :] for k in range(4)], axis=1)
            valid = jnp.concatenate(
                [cmask_ref[4 * g + k : 4 * g + k + 1, :] for k in range(4)], axis=1
            ).astype(F32)
            hot = one_hot((ids + C * d) & 255, 2 * C)
            total += message(dot(proj, hot), own4, wts[6 * layer + 2], bias1, valid)
        total = (total[:, 0:C] + total[:, C : 2 * C]) + (
            total[:, 2 * C : 3 * C] + total[:, 3 * C :]
        )
        return node_update(
            rows,
            node_part,
            total,
            wts[6 * layer + 4],
            wts[6 * layer + 5],
            bias(layer, 3, True),
        )

    prepare(0)
    rows = x.T
    fine_ref[...] = fine_layer(0, rows, split(rows), rims, rim_recv)

    weighted = split(fine_ref[...] * share)
    side_send[...] = fold_lanes(dot_nt(side_pick[...], weighted))
    low_rows = side_send.at[pl.ds(0, SIDE)]
    high_rows = side_send.at[pl.ds(SIDE, SIDE)]
    sides = side_copies(8, ((low_rows, low_rows), (high_rows, high_rows)), side_recv)
    for c in sides:
        c.start()
    partial = fold(dot_nt(weighted, own_hot[...]))
    part_send[:, 0:C] = partial[:, C:]
    part_send[:, C:] = partial[:, 0:C]
    part_copy = copy(12, part_send, part_recv, (r, other))
    part_copy.start()

    prepare(1)
    prepare(2)
    prepare(3)
    for c in side_arrivals(3, low_meta, meta_recv):
        c.wait_recv()
    tot_copy.wait_recv()
    facts_in = meta_recv[...].reshape(4 * SIDE, W)
    p_in = (facts_in[:, 0:1].astype(jnp.int32) + C * d) & 255
    match = lax.broadcasted_iota(jnp.int32, (4 * SIDE, 2 * C), 1) == p_in
    side_hot = match.astype(F32).astype(BF16)
    side_total = jnp.sum(jnp.where(match, facts_in[:, 64:65], 0.0), axis=0, keepdims=True)
    totals = own_total[0:1] + tot_recv[0:1, :] + side_total
    inverse = 1.0 / jnp.maximum(totals, 1.0)

    for c in side_arrivals(8, low_rows, side_recv):
        c.wait_recv()
    from_sides = fold(dot(split(side_recv[...].reshape(4 * SIDE, W).T), side_hot))
    part_copy.wait_recv()
    coarse = (partial + part_recv[...] + from_sides) * inverse

    group = split(coarse)
    mid = coarse_layer(1, coarse[:, 0:C], group[:, 0:C], lambda: group)
    mid_send[...] = mid
    mid_copy = copy(13, mid_send, mid_recv, (r, other))
    mid_copy.start()
    mid_split = split(mid)

    def mid_sources():
        mid_copy.wait_recv()
        return jnp.concatenate([mid_split, split(mid_recv[...])], axis=1)

    coarse_out = coarse_layer(2, mid, mid_split, mid_sources)
    co_split = split(coarse_out)
    reply_send[...] = fold_lanes(dot_nt(side_hot[:, 0:C], co_split)).reshape(4, SIDE, W)
    replies = side_copies(
        14,
        ((reply_send.at[0], reply_send.at[1]), (reply_send.at[2], reply_send.at[3])),
        reply_recv,
    )
    for c in replies:
        c.start()
    co_send[...] = coarse_out
    co_copy = copy(18, co_send, co_recv, (r, other))
    co_copy.start()
    cout_ref[...] = coarse_out.T

    co_copy.wait_recv()
    known = jnp.concatenate([co_split, split(co_recv[...])], axis=1)
    added = fold(dot(known, own_hot[...]))
    for c in side_arrivals(14, reply_send.at[0], reply_recv):
        c.wait_recv()
    back = jnp.concatenate(
        [reply_recv[0] + reply_recv[1], reply_recv[2] + reply_recv[3]], axis=0
    )
    added += fold(dot(split(back.T), side_pick[...]))
    rows = fine_ref[...] + (share * 0.25) * added
    rows_split = split(rows)
    rim2_send[...] = fold_lanes(dot_nt(rim_pick[...], rows_split))
    rims2 = rim_copies(19, rim2_send, rim2_recv)
    for c in rims2:
        c.start()
    out_ref[...] = fine_layer(3, rows, rows_split, rims2, rim2_recv).T

    for c in rims + metas + [tot_copy] + sides + [part_copy, mid_copy] + replies + [co_copy] + rims2:
        c.wait_send()


def body(regions, *args):
    vmem = pl.BlockSpec(memory_space=pltpu.VMEM)
    return pl.pallas_call(
        functools.partial(kernel, regions),
        out_shape=(
            jax.ShapeDtypeStruct((F, W), F32),
            jax.ShapeDtypeStruct((C, W), F32),
        ),
        in_specs=[vmem] * 11,
        out_specs=(vmem, vmem),
        scratch_shapes=[
            pltpu.VMEM((W, W), F32),
            pltpu.VMEM((24, 2 * W, 2 * W), BF16),
            pltpu.VMEM((2 * W, F + 4 * H), BF16),
            pltpu.VMEM((W, F), F32),
            pltpu.VMEM((W, F), F32),
            pltpu.VMEM((W, F), F32),
            pltpu.VMEM((W, F), F32),
            pltpu.VMEM((4 * H, F), BF16),
            pltpu.VMEM((2 * SIDE, F), BF16),
            pltpu.VMEM((2 * C, F), BF16),
            pltpu.VMEM((4 * H, W), F32),
            pltpu.VMEM((4 * H, W), F32),
            pltpu.VMEM((2 * SIDE, W), F32),
            pltpu.VMEM((4, SIDE, W), F32),
            pltpu.VMEM((8, 2 * C), F32),
            pltpu.VMEM((8, 2 * C), F32),
            pltpu.VMEM((W, 2 * C), F32),
            pltpu.VMEM((W, 2 * C), F32),
            pltpu.VMEM((2 * SIDE, W), F32),
            pltpu.VMEM((4, SIDE, W), F32),
            pltpu.VMEM((W, C), F32),
            pltpu.VMEM((W, C), F32),
            pltpu.VMEM((W, C), F32),
            pltpu.VMEM((W, C), F32),
            pltpu.VMEM((4, SIDE, W), F32),
            pltpu.VMEM((4, SIDE, W), F32),
            pltpu.VMEM((4 * H, W), F32),
            pltpu.VMEM((4 * H, W), F32),
            pltpu.SemaphoreType.DMA((22,)),
            pltpu.SemaphoreType.DMA((22,)),
        ],
        compiler_params=pltpu.CompilerParams(collective_id=0, has_side_effects=True),
    )(*args)


def solution(mesh):
    both = ("region", "dom")
    return jax.shard_map(
        functools.partial(body, mesh.shape["region"]),
        mesh=mesh,
        in_specs=(
            P(both, None),
            P(None, both),
            P(None, both),
            P(None, both),
            P(None, both),
            P(None, both),
            P(both),
            P(both),
            P(),
            P(),
            P(),
        ),
        out_specs=(P(both, None), P(both, None)),
        check_vma=False,
    )
```

profile of v0, /device:TPU:1, one launch (start us, length us, event | category | flops | bytes accessed | tf_op | source)
XLA Modules:
  0.0 71.1 jit_solution(6636214159598286610)
XLA Ops:
  0.6 68.1 %shard_map.122 = (f32[512,128]{1,0:T(8,128)}, f32[128,128]{1,0:T(8,128)}) custom-call(f32[512,128]{1,0:T(8,128)} %x_ref.1, s32[16,512]{1,0:T(8,128)} %nbr_ref.1, s32[16,512]{1,0:T(8,128)} %mask_ref.1, s32[4,16]{1,0:T(4,128)} %send_ref.1, s32[16,128]{1,0:T(8,128)} %cnbr_ref.1, s32[16,128]{1,0:T(8,128)} %cmask_ref.1, s32[512]{0:T(512)} %parent_ref.1, ...), custom_call_target="tpu_custom_call" | custom-call | tf_op jit(solution)/shard_map/pallas_call | solution.py:387
  68.8 0.0 copy-start
  68.8 1.7 %copy.15 = f32[512,128]{1,0:T(8,128)} copy(f32[512,128]{1,0:T(8,128)} %get-tuple-element.4) | data formatting | bytes 524288
  70.5 0.0 copy-done
  70.5 0.6 copy.16
Async XLA Ops:
  68.8 1.7 %copy-start = (f32[128,128]{1,0:T(8,128)S(1)}, f32[128,128]{1,0:T(8,128)}, u32[]{:S(2)}) copy-start(f32[128,128]{1,0:T(8,128)} %get-tuple-element.5) | copy-start | bytes 196612
where the time goes:
time: 71.3 us; the launch traced here: 71.1 us
  Pallas kernels  68.1 us (96%)
  local copies, waits for them, and re-layouts  2.33 us (3%)
    pallas_call x1, Pallas kernels, body(): pl.pallas_call(functools.partial(kernel, regions), out_shape=(jax.ShapeDt...  68.1 us
    unnamed x4, local copies, waits for them, and re-layouts  2.33 us

commit v1 on v0

--- a/solution.py
+++ b/solution.py
@@ -50,8 +50,9 @@
     blocks = []
     for base in range(0, depth, 256):
         size = min(256, depth - base)
-        rows = lax.broadcasted_iota(jnp.int32, (size, n), 0)
-        blocks.append((rows == (index_row - base)).astype(F32).astype(BF16))
+        rows = lax.broadcasted_iota(jnp.int32, (size, n), 0).astype(F32).astype(BF16)
+        wanted = (index_row - base).astype(F32).astype(BF16)
+        blocks.append(jnp.where(rows == wanted, jnp.ones((), BF16), jnp.zeros((), BF16)))
     return blocks[0] if len(blocks) == 1 else jnp.concatenate(blocks, axis=0)
 
 
@@ -71,8 +72,8 @@
     return column - jnp.sum(column, axis=0, keepdims=True) * (1.0 / W)
 
 
-def message(gathered, own, second, second_bias, valid_row):
-    hidden = jnp.maximum(fold(gathered) + own, 0.0)
+def message(hidden, second, second_bias, valid_row):
+    hidden = jnp.maximum(hidden, 0.0)
     centred = fold(dot(second, split(hidden))) + second_bias
     return centred * (scale_of(centred) * valid_row)
 
@@ -85,6 +86,19 @@
 
 def kernel(
     regions,
+    x_in,
+    nbr_in,
+    mask_in,
+    send_in,
+    cnbr_in,
+    cmask_in,
+    parent_in,
+    share_in,
+    edge_in,
+    node_in,
+    bias_in,
+    out_ref,
+    cout_ref,
     x_ref,
     nbr_ref,
     mask_ref,
@@ -96,10 +110,9 @@
     edge_ref,
     node_ref,
     bias_ref,
-    out_ref,
-    cout_ref,
     tile_ref,
     wts,
+    base_ref,
     src_proj,
     own_ref,
     node_own,
@@ -128,6 +141,7 @@
     rim2_recv,
     send_sem,
     recv_sem,
+    load_sem,
 ):
     r = lax.axis_index("region")
     d = lax.axis_index("dom")
@@ -138,6 +152,29 @@
     barrier = pltpu.get_barrier_semaphore()
     for peer in peers:
         pl.semaphore_signal(barrier, inc=1, device_id=peer, device_id_type=MESH)
+
+    loads = [
+        pltpu.make_async_copy(src, dst, load_sem.at[k])
+        for k, (src, dst) in enumerate(
+            (
+                (send_in, send_ref),
+                (x_in, x_ref),
+                (parent_in, parent_ref),
+                (share_in, share_ref),
+                (edge_in.at[0], edge_ref.at[0]),
+                (node_in.at[0], node_ref.at[0]),
+                (bias_in, bias_ref),
+                (nbr_in, nbr_ref),
+                (mask_in, mask_ref),
+                (cnbr_in, cnbr_ref),
+                (cmask_in, cmask_ref),
+                (edge_in.at[pl.ds(1, 3)], edge_ref.at[pl.ds(1, 3)]),
+                (node_in.at[pl.ds(1, 3)], node_ref.at[pl.ds(1, 3)]),
+            )
+        )
+    ]
+    for c in loads:
+        c.start()
 
     def copy(k, src, dst, peer):
         return pltpu.make_async_remote_copy(
@@ -177,6 +214,7 @@
         return [copy(base + k, src, dst.at[k], (r, other)) for k in range(4)]
 
     tile_ref[...] = jnp.zeros_like(tile_ref)
+    loads[0].wait()
     tile_ref[0:4, 0:H] = send_ref[...].astype(F32)
     lists = tile_ref[...].T
     lane = lax.broadcasted_iota(jnp.int32, (H, F), 1)
@@ -186,15 +224,13 @@
         picks.append((lane == column).astype(F32).astype(BF16))
     rim_pick[...] = jnp.concatenate(picks, axis=0)
 
+    loads[1].wait()
     x = x_ref[...]
     x_hi, x_lo = halves(x)
     rim_send[...] = dot(rim_pick[...], x_hi) + dot(rim_pick[...], x_lo)
 
-    pl.semaphore_wait(barrier, 5)
-    rims = rim_copies(0, rim_send, rim_recv)
-    for c in rims:
-        c.start()
-
+    loads[2].wait()
+    loads[3].wait()
     parent = parent_ref[...].reshape(1, F)
     share = share_ref[...].reshape(1, F).astype(F32)
     p_region = lax.shift_right_logical(parent, 8)
@@ -223,15 +259,19 @@
     low_meta = meta_send.at[pl.ds(0, SIDE)]
     high_meta = meta_send.at[pl.ds(SIDE, SIDE)]
     metas = side_copies(3, ((low_meta, low_meta), (high_meta, high_meta)), meta_recv)
-    for c in metas:
-        c.start()
     shares16 = jnp.broadcast_to(share, (16, F)).astype(BF16)
     own_total = dot_nt(shares16, own_hot[...])[0:8]
     tot_send[:, 0:C] = own_total[:, C:]
     tot_send[:, C:] = own_total[:, 0:C]
     tot_copy = copy(7, tot_send, tot_recv, (r, other))
-    tot_copy.start()
-
+
+    pl.semaphore_wait(barrier, 5)
+    rims = rim_copies(0, rim_send, rim_recv)
+    for c in rims + metas + [tot_copy]:
+        c.start()
+
+    for c in loads[4:9]:
+        c.wait()
     tile_ref[0:16, :] = bias_ref[...].reshape(16, W)
     biases = tile_ref[...].T
 
@@ -244,29 +284,89 @@
             wts[6 * layer + k] = stacked(edge_ref[layer, k], centred=k == 2)
             wts[6 * layer + 3 + k] = stacked(node_ref[layer, k], centred=k == 2)
 
-    def fine_layer(layer, rows, rows_split, rim_arrivals, rim_rows):
+    side_twice = jnp.concatenate([side_pick[...], side_pick[...]], axis=0)
+
+    def fine_own(layer, rows_split):
         own_ref[...] = fold(dot(wts[6 * layer], rows_split)) + bias(layer, 0)
         node_own[...] = fold(dot(wts[6 * layer + 3], rows_split)) + bias(layer, 2)
         src_proj[:, 0:F] = split(fold(dot(wts[6 * layer + 1], rows_split)))
+
+        def slot(s, carry):
+            hot = one_hot(nbr_ref[pl.ds(s, 1), :], F)
+            base_ref[s] = fold(dot(src_proj[:, 0:F], hot)) + own_ref[...]
+            return carry
+
+        lax.fori_loop(0, SLOTS, slot, 0, unroll=4)
+
+    def fine_rims(layer, rim_arrivals, rim_rows):
         for c in rim_arrivals:
             c.wait_recv()
         rim = jnp.concatenate(halves(rim_rows[...]), axis=1)
         src_proj[:, F:] = split(fold(dot_nt(wts[6 * layer + 1], rim)))
+
+    def fine_messages(layer, rows):
         total_ref[...] = jnp.zeros_like(total_ref)
         bias1 = jnp.broadcast_to(bias(layer, 1, True), (W, F))
 
-        def slot(s, carry):
-            hot = one_hot(nbr_ref[pl.ds(s, 1), :], F + 4 * H)
-            gathered = dot(src_proj[...], hot)
-            valid = mask_ref[pl.ds(s, 1), :].astype(F32)
-            total_ref[...] += message(gathered, own_ref[...], wts[6 * layer + 2], bias1, valid)
+        def slots(g, carry):
+            rows4 = [8 * g + k for k in range(8)]
+            for t in range(0, F, 256):
+                cols = pl.ds(t, 256)
+                total = total_ref[:, cols]
+                hidden = [
+                    base_ref[s, :, cols]
+                    + fold(dot(src_proj[:, F:], one_hot(nbr_ref[pl.ds(s, 1), cols] - F, 4 * H)))
+                    for s in rows4
+                ]
+                hidden = [split(jnp.maximum(h, 0.0)) for h in hidden]
+                centred = [fold(dot(wts[6 * layer + 2], h)) + bias1[:, 0:256] for h in hidden]
+                scales = [
+                    scale_of(c) * mask_ref[pl.ds(s, 1), cols].astype(F32) for c, s in zip(centred, rows4)
+                ]
+                for c, scale in zip(centred, scales):
+                    total = total + c * scale
+                total_ref[:, cols] = total
             return carry
 
-        lax.fori_loop(0, SLOTS, slot, 0)
+        lax.fori_loop(0, SLOTS // 8, slots, 0, unroll=1)
         return node_update(
             rows,
             node_own[...],
             total_ref[...],
+            wts[6 * layer + 4],
+            wts[6 * layer + 5],
+            bias(layer, 3, True),
+        )
+
+    def picked(values):
+        return fold(dot_nt(split(values), side_twice))
+
+    def paired(table):
+        parts = jnp.concatenate([table & -16, table & 15], axis=0).astype(F32).astype(BF16)
+        both = dot_nt(parts, side_twice)
+        values = (both[0:SLOTS] + both[SLOTS:]).astype(jnp.int32)
+        first = lax.broadcasted_iota(jnp.int32, (8, W), 1) < 2 * SIDE
+        return jnp.where(first, values[0:8], values[8:16])
+
+    def side_nodes(layer, rows):
+        ids8 = paired(nbr_ref[...])
+        valid8 = paired(mask_ref[...]).astype(F32)
+        own4 = jnp.concatenate([picked(own_ref[...])] * 4, axis=1)
+        bias1 = jnp.broadcast_to(bias(layer, 1, True), (W, 4 * W))
+        total = jnp.zeros((W, 4 * W), F32)
+        for g in range(2):
+            ids = jnp.concatenate([ids8[4 * g + k : 4 * g + k + 1] for k in range(4)], axis=1)
+            valid = jnp.concatenate([valid8[4 * g + k : 4 * g + k + 1] for k in range(4)], axis=1)
+            hidden = fold(dot(src_proj[...], one_hot(ids, F + 4 * H))) + own4
+            total += message(hidden, wts[6 * layer + 2], bias1, valid)
+        total = (total[:, 0:W] + total[:, W : 2 * W]) + (
+            total[:, 2 * W : 3 * W] + total[:, 3 * W :]
+        )
+        total = total + pltpu.roll(total, 2 * SIDE, 1)
+        return node_update(
+            picked(rows),
+            picked(node_own[...]),
+            total,
             wts[6 * layer + 4],
             wts[6 * layer + 5],
             bias(layer, 3, True),
@@ -285,7 +385,7 @@
                 [cmask_ref[4 * g + k : 4 * g + k + 1, :] for k in range(4)], axis=1
             ).astype(F32)
             hot = one_hot((ids + C * d) & 255, 2 * C)
-            total += message(dot(proj, hot), own4, wts[6 * layer + 2], bias1, valid)
+            total += message(fold(dot(proj, hot)) + own4, wts[6 * layer + 2], bias1, valid)
         total = (total[:, 0:C] + total[:, C : 2 * C]) + (
             total[:, 2 * C : 3 * C] + total[:, 3 * C :]
         )
@@ -300,24 +400,30 @@
 
     prepare(0)
     rows = x.T
-    fine_ref[...] = fine_layer(0, rows, split(rows), rims, rim_recv)
-
-    weighted = split(fine_ref[...] * share)
-    side_send[...] = fold_lanes(dot_nt(side_pick[...], weighted))
+    fine_own(0, split(rows))
+    for c in loads[9:]:
+        c.wait()
+    prepare(1)
+    prepare(2)
+    prepare(3)
+    fine_rims(0, rims, rim_recv)
+
+    side_share = dot_nt(shares16, side_twice)[0:1]
+    side_send[...] = (side_nodes(0, rows) * side_share).T[0 : 2 * SIDE]
     low_rows = side_send.at[pl.ds(0, SIDE)]
     high_rows = side_send.at[pl.ds(SIDE, SIDE)]
     sides = side_copies(8, ((low_rows, low_rows), (high_rows, high_rows)), side_recv)
     for c in sides:
         c.start()
+    fine_ref[...] = fine_messages(0, rows)
+
+    weighted = split(fine_ref[...] * share)
     partial = fold(dot_nt(weighted, own_hot[...]))
     part_send[:, 0:C] = partial[:, C:]
     part_send[:, C:] = partial[:, 0:C]
     part_copy = copy(12, part_send, part_recv, (r, other))
     part_copy.start()
 
-    prepare(1)
-    prepare(2)
-    prepare(3)
     for c in side_arrivals(3, low_meta, meta_recv):
         c.wait_recv()
     tot_copy.wait_recv()
@@ -376,7 +482,9 @@
     rims2 = rim_copies(19, rim2_send, rim2_recv)
     for c in rims2:
         c.start()
-    out_ref[...] = fine_layer(3, rows, rows_split, rims2, rim2_recv).T
+    fine_own(3, rows_split)
+    fine_rims(3, rims2, rim2_recv)
+    out_ref[...] = fine_messages(3, rows).T
 
     for c in rims + metas + [tot_copy] + sides + [part_copy, mid_copy] + replies + [co_copy] + rims2:
         c.wait_send()
@@ -390,11 +498,13 @@
             jax.ShapeDtypeStruct((F, W), F32),
             jax.ShapeDtypeStruct((C, W), F32),
         ),
-        in_specs=[vmem] * 11,
+        in_specs=[pl.BlockSpec(memory_space=pl.ANY)] * 11,
         out_specs=(vmem, vmem),
-        scratch_shapes=[
+        scratch_shapes=[pltpu.VMEM(a.shape, a.dtype) for a in args]
+        + [
             pltpu.VMEM((W, W), F32),
             pltpu.VMEM((24, 2 * W, 2 * W), BF16),
+            pltpu.VMEM((SLOTS, W, F), F32),
             pltpu.VMEM((2 * W, F + 4 * H), BF16),
             pltpu.VMEM((W, F), F32),
             pltpu.VMEM((W, F), F32),
@@ -423,6 +533,7 @@
             pltpu.VMEM((4 * H, W), F32),
             pltpu.SemaphoreType.DMA((22,)),
             pltpu.SemaphoreType.DMA((22,)),
+            pltpu.SemaphoreType.DMA((13,)),
         ],
         compiler_params=pltpu.CompilerParams(collective_id=0, has_side_effects=True),
     )(*args)

time: 71.3 us -> 52.3 us (0.73)
  Pallas kernels: 68.1 us -> 49.2 us
    pallas_call x1, Pallas kernels: 68.1 us -> 49.2 us  [body(): pl.pallas_call(functools.partial(kernel, regions), out_shape=(jax.ShapeDt...]
where the time goes in v1:
time: 52.3 us; the launch traced here: 52.2 us
  Pallas kernels  49.2 us (94%)
  local copies, waits for them, and re-layouts  2.33 us (4%)
  between operations  0.65 us (1%)
    pallas_call x1, Pallas kernels, body(): pl.pallas_call(functools.partial(kernel, regions), out_shape=(jax.ShapeDt...  49.2 us
    unnamed x4, local copies, waits for them, and re-layouts  2.33 us

profile of v1, /device:TPU:1, one launch (start us, length us, event | category | flops | bytes accessed | tf_op | source)
XLA Modules:
  0.0 52.2 jit_solution(15203411746755718770)
XLA Ops:
  0.6 49.2 %shard_map.122 = (f32[512,128]{1,0:T(8,128)}, f32[128,128]{1,0:T(8,128)}) custom-call(f32[512,128]{1,0:T(8,128)} %x_in.1, s32[16,512]{1,0:T(8,128)} %nbr_in.1, s32[16,512]{1,0:T(8,128)} %mask_in.1, s32[4,16]{1,0:T(4,128)} %send_in.1, s32[16,128]{1,0:T(8,128)} %cnbr_in.1, s32[16,128]{1,0:T(8,128)} %cmask_in.1, s32[512]{0:T(512)} %parent_in.1, s32[512]{0:T(512)} %share_in.1, ...), custom_call_target="tpu_custom_call" | custom-call | tf_op jit(solution)/shard_map/pallas_call | solution.py:495
  49.8 0.0 copy-start
  49.8 1.7 %copy.15 = f32[512,128]{1,0:T(8,128)} copy(f32[512,128]{1,0:T(8,128)} %get-tuple-element.4) | data formatting | bytes 524288
  51.5 0.0 copy-done
  51.5 0.6 %copy.16 = f32[128,128]{1,0:T(8,128)} copy(f32[128,128]{1,0:T(8,128)S(1)} %copy-done) | data formatting | bytes 131072
Async XLA Ops:
  49.8 1.7 %copy-start = (f32[128,128]{1,0:T(8,128)S(1)}, f32[128,128]{1,0:T(8,128)}, u32[]{:S(2)}) copy-start(f32[128,128]{1,0:T(8,128)} %get-tuple-element.5) | copy-start | bytes 196612

commit v2 on v1

--- a/solution.py
+++ b/solution.py
@@ -118,9 +118,9 @@
     node_own,
     total_ref,
     fine_ref,
-    rim_pick,
-    side_pick,
+    pick_all,
     own_hot,
+    side_ids,
     rim_send,
     rim_recv,
     meta_send,
@@ -135,8 +135,8 @@
     mid_recv,
     co_send,
     co_recv,
-    reply_send,
-    reply_recv,
+    pay_send,
+    pay_recv,
     rim2_send,
     rim2_recv,
     send_sem,
@@ -148,7 +148,9 @@
     up = lax.rem(r + 1, regions)
     down = lax.rem(r + regions - 1, regions)
     other = 1 - d
-    peers = [(down, 0), (down, 1), (up, 0), (up, 1), (r, other)]
+    up2 = lax.rem(r + 2, regions)
+    down2 = lax.rem(r + regions - 2, regions)
+    peers = [(down, d), (down, other), (up, d), (up, other), (r, other), (up2, d), (down2, d)]
     barrier = pltpu.get_barrier_semaphore()
     for peer in peers:
         pl.semaphore_signal(barrier, inc=1, device_id=peer, device_id_type=MESH)
@@ -193,24 +195,21 @@
             copy(base + 2, src.at[pl.ds(2 * H, 2 * H)], dst.at[pl.ds(2 * H, 2 * H)], (r, other)),
         ]
 
-    def side_copies(base, src, dst):
-        copies = []
-        for way, region in ((0, down), (1, up)):
-            for e in range(2):
-                copies.append((way, e, region))
+    def four_copies(base, low, high, dst):
         return [
             pltpu.make_async_remote_copy(
-                src_ref=src[way][e],
-                dst_ref=dst.at[2 * (1 - way) + d],
-                send_sem=send_sem.at[base + 2 * way + e],
-                recv_sem=recv_sem.at[base + 2 * (1 - way) + d],
-                device_id=(region, e),
+                src_ref=src,
+                dst_ref=dst.at[2 * (1 - way) + cross],
+                send_sem=send_sem.at[base + 2 * way + cross],
+                recv_sem=recv_sem.at[base + 2 * (1 - way) + cross],
+                device_id=(region, other if cross else d),
                 device_id_type=MESH,
             )
-            for way, e, region in copies
+            for way, src, region in ((0, low, down), (1, high, up))
+            for cross in range(2)
         ]
 
-    def side_arrivals(base, src, dst):
+    def four_arrivals(base, src, dst):
         return [copy(base + k, src, dst.at[k], (r, other)) for k in range(4)]
 
     tile_ref[...] = jnp.zeros_like(tile_ref)
@@ -222,12 +221,12 @@
     for j in range(4):
         column = lists[0:H, j : j + 1].astype(jnp.int32)
         picks.append((lane == column).astype(F32).astype(BF16))
-    rim_pick[...] = jnp.concatenate(picks, axis=0)
+    pick_all[2 * SIDE :, :] = jnp.concatenate(picks, axis=0)
 
     loads[1].wait()
     x = x_ref[...]
     x_hi, x_lo = halves(x)
-    rim_send[...] = dot(rim_pick[...], x_hi) + dot(rim_pick[...], x_lo)
+    rim_send[...] = dot(pick_all[2 * SIDE :, :], x_hi) + dot(pick_all[2 * SIDE :, :], x_lo)
 
     loads[2].wait()
     loads[3].wait()
@@ -246,26 +245,29 @@
         jnp.int32, (F, F), 1
     )
     ranks = dot(flags, before.astype(F32).astype(BF16)).astype(jnp.int32) - 1
-    side_pick[...] = jnp.concatenate(
-        [
-            one_hot(jnp.where(at_low, ranks[0:1], -1), SIDE),
-            one_hot(jnp.where(at_high, ranks[1:2], -1), SIDE),
-        ],
-        axis=0,
+    low_rank = jnp.where(at_low, ranks[0:1], -1)
+    high_rank = jnp.where(at_high, ranks[1:2], -1)
+    pick_all[0 : 2 * SIDE, :] = jnp.concatenate(
+        [one_hot(low_rank, SIDE), one_hot(high_rank, SIDE)], axis=0
     )
-    sub = lax.broadcasted_iota(jnp.int32, (W, F), 0)
-    facts = jnp.where(sub < 64, p_local.astype(F32), share).astype(BF16)
-    meta_send[...] = dot_nt(side_pick[...], facts)
-    low_meta = meta_send.at[pl.ds(0, SIDE)]
-    high_meta = meta_send.at[pl.ds(SIDE, SIDE)]
-    metas = side_copies(3, ((low_meta, low_meta), (high_meta, high_meta)), meta_recv)
+    side_pick = pick_all.at[pl.ds(0, 2 * SIDE)]
+    rim_pick = pick_all.at[pl.ds(2 * SIDE, 4 * H)]
+    number = jnp.where(at_high, high_rank + SIDE, low_rank) + 1
+    src_proj[2 * W :, 0:F] = jnp.broadcast_to(number.astype(F32), (16, F)).astype(BF16)
+    where_at = at_low.astype(F32) + 2.0 * at_high.astype(F32)
+    facts = jnp.concatenate(
+        [p_local.astype(F32), share, where_at, jnp.zeros((13, F), F32)], axis=0
+    ).astype(BF16)
+    meta_send[...] = dot_nt(facts, pick_all[...])[0:8]
+    metas = four_copies(3, meta_send, meta_send, meta_recv)
+    metas.append(copy(7, meta_send, meta_recv.at[4], (r, other)))
     shares16 = jnp.broadcast_to(share, (16, F)).astype(BF16)
     own_total = dot_nt(shares16, own_hot[...])[0:8]
     tot_send[:, 0:C] = own_total[:, C:]
     tot_send[:, C:] = own_total[:, 0:C]
-    tot_copy = copy(7, tot_send, tot_recv, (r, other))
-
-    pl.semaphore_wait(barrier, 5)
+    tot_copy = copy(8, tot_send, tot_recv, (r, other))
+
+    pl.semaphore_wait(barrier, 7)
     rims = rim_copies(0, rim_send, rim_recv)
     for c in rims + metas + [tot_copy]:
         c.start()
@@ -289,11 +291,16 @@
     def fine_own(layer, rows_split):
         own_ref[...] = fold(dot(wts[6 * layer], rows_split)) + bias(layer, 0)
         node_own[...] = fold(dot(wts[6 * layer + 3], rows_split)) + bias(layer, 2)
-        src_proj[:, 0:F] = split(fold(dot(wts[6 * layer + 1], rows_split)))
+        src_proj[0 : 2 * W, 0:F] = split(fold(dot(wts[6 * layer + 1], rows_split)))
 
         def slot(s, carry):
             hot = one_hot(nbr_ref[pl.ds(s, 1), :], F)
-            base_ref[s] = fold(dot(src_proj[:, 0:F], hot)) + own_ref[...]
+            if layer == 0:
+                gathered = dot(src_proj[:, 0:F], hot)
+                side_ids[pl.ds(s, 1), :] = gathered[2 * W : 2 * W + 1].astype(jnp.int32) - 1
+            else:
+                gathered = dot(src_proj[0 : 2 * W, 0:F], hot)
+            base_ref[s] = fold(gathered[0 : 2 * W]) + own_ref[...]
             return carry
 
         lax.fori_loop(0, SLOTS, slot, 0, unroll=4)
@@ -302,9 +309,9 @@
         for c in rim_arrivals:
             c.wait_recv()
         rim = jnp.concatenate(halves(rim_rows[...]), axis=1)
-        src_proj[:, F:] = split(fold(dot_nt(wts[6 * layer + 1], rim)))
-
-    def fine_messages(layer, rows):
+        src_proj[0 : 2 * W, F:] = split(fold(dot_nt(wts[6 * layer + 1], rim)))
+
+    def fine_messages(layer, rows, extra_proj, extra_hot):
         total_ref[...] = jnp.zeros_like(total_ref)
         bias1 = jnp.broadcast_to(bias(layer, 1, True), (W, F))
 
@@ -315,7 +322,7 @@
                 total = total_ref[:, cols]
                 hidden = [
                     base_ref[s, :, cols]
-                    + fold(dot(src_proj[:, F:], one_hot(nbr_ref[pl.ds(s, 1), cols] - F, 4 * H)))
+                    + fold(dot(extra_proj, extra_hot(s, cols)))
                     for s in rows4
                 ]
                 hidden = [split(jnp.maximum(h, 0.0)) for h in hidden]
@@ -357,7 +364,7 @@
         for g in range(2):
             ids = jnp.concatenate([ids8[4 * g + k : 4 * g + k + 1] for k in range(4)], axis=1)
             valid = jnp.concatenate([valid8[4 * g + k : 4 * g + k + 1] for k in range(4)], axis=1)
-            hidden = fold(dot(src_proj[...], one_hot(ids, F + 4 * H))) + own4
+            hidden = fold(dot(src_proj[0 : 2 * W, :], one_hot(ids, F + 4 * H))) + own4
             total += message(hidden, wts[6 * layer + 2], bias1, valid)
         total = (total[:, 0:W] + total[:, W : 2 * W]) + (
             total[:, 2 * W : 3 * W] + total[:, 3 * W :]
@@ -378,14 +385,19 @@
         proj = split(fold(dot(wts[6 * layer + 1], sources())))
         own4 = jnp.concatenate([own] * 4, axis=1)
         bias1 = jnp.broadcast_to(bias(layer, 1, True), (W, 4 * C))
-        total = jnp.zeros((W, 4 * C), F32)
+        id_rows, valid_rows = [], []
         for g in range(4):
-            ids = jnp.concatenate([cnbr_ref[4 * g + k : 4 * g + k + 1, :] for k in range(4)], axis=1)
-            valid = jnp.concatenate(
-                [cmask_ref[4 * g + k : 4 * g + k + 1, :] for k in range(4)], axis=1
-            ).astype(F32)
-            hot = one_hot((ids + C * d) & 255, 2 * C)
-            total += message(fold(dot(proj, hot)) + own4, wts[6 * layer + 2], bias1, valid)
+            k = range(4 * g, 4 * g + 4)
+            id_rows.append(jnp.concatenate([cnbr_ref[i : i + 1, :] for i in k], axis=1))
+            valid_rows.append(
+                jnp.concatenate([cmask_ref[i : i + 1, :] for i in k], axis=1).astype(F32)
+            )
+        hots = [one_hot((ids + C * d) & 255, 2 * C) for ids in id_rows]
+        hidden = [split(jnp.maximum(fold(dot(proj, hot)) + own4, 0.0)) for hot in hots]
+        centred = [fold(dot(wts[6 * layer + 2], h)) + bias1 for h in hidden]
+        scales = [scale_of(c) * valid for c, valid in zip(centred, valid_rows)]
+        total = centred[0] * scales[0] + centred[1] * scales[1]
+        total = total + (centred[2] * scales[2] + centred[3] * scales[3])
         total = (total[:, 0:C] + total[:, C : 2 * C]) + (
             total[:, 2 * C : 3 * C] + total[:, 3 * C :]
         )
@@ -412,30 +424,62 @@
     side_send[...] = (side_nodes(0, rows) * side_share).T[0 : 2 * SIDE]
     low_rows = side_send.at[pl.ds(0, SIDE)]
     high_rows = side_send.at[pl.ds(SIDE, SIDE)]
-    sides = side_copies(8, ((low_rows, low_rows), (high_rows, high_rows)), side_recv)
+    sides = four_copies(9, low_rows, high_rows, side_recv)
     for c in sides:
         c.start()
-    fine_ref[...] = fine_messages(0, rows)
+    def rim_hot(s, cols):
+        return one_hot(nbr_ref[pl.ds(s, 1), cols] - F, 4 * H)
+
+    fine_ref[...] = fine_messages(0, rows, src_proj[0 : 2 * W, F:], rim_hot)
 
     weighted = split(fine_ref[...] * share)
     partial = fold(dot_nt(weighted, own_hot[...]))
     part_send[:, 0:C] = partial[:, C:]
     part_send[:, C:] = partial[:, 0:C]
-    part_copy = copy(12, part_send, part_recv, (r, other))
+    part_copy = copy(13, part_send, part_recv, (r, other))
     part_copy.start()
 
-    for c in side_arrivals(3, low_meta, meta_recv):
+    rim2_send[...] = fold_lanes(dot_nt(rim_pick[...], split(fine_ref[...])))
+    rims2 = rim_copies(20, rim2_send, rim2_recv)
+    for c in rims2:
+        c.start()
+
+    for c in four_arrivals(3, meta_send, meta_recv) + metas[4:]:
         c.wait_recv()
+    tile_ref[0:40, :] = meta_recv[...].reshape(40, W)
+    tile_ref[40:48, :] = meta_send[...]
+    lists = tile_ref[...].T
+
+    def listed(k, start, size, only=None):
+        rows_at = slice(start, start + size)
+        weight = lists[rows_at, 8 * k + 1 : 8 * k + 2]
+        if only is not None:
+            weight = jnp.where(lists[rows_at, 8 * k + 2 : 8 * k + 3] == only, weight, 0.0)
+        return lists[rows_at, 8 * k : 8 * k + 1], weight
+
+    def chosen(entries):
+        wanted = jnp.concatenate([e[0] for e in entries], axis=0).astype(jnp.int32)
+        weight = jnp.concatenate([e[1] for e in entries], axis=0)
+        nodes = lax.broadcasted_iota(jnp.int32, (wanted.shape[0], 2 * C), 1)
+        return nodes == ((wanted + C * d) & 255), weight
+
+    match, weight_in = chosen(
+        [listed(0, 32, 32), listed(1, 32, 32), listed(2, 0, 32), listed(3, 0, 32)]
+    )
+    side_hot = match.astype(F32).astype(BF16)
+    side_total = jnp.sum(jnp.where(match, weight_in, 0.0), axis=0, keepdims=True)
+    match, weight_out = chosen(
+        [listed(2, 0, 32), listed(3, 96, 32, 1.0), listed(5, 64, 16, 0.0)]
+        + [listed(0, 32, 32), listed(1, 96, 32, 2.0), listed(5, 80, 16, 0.0)]
+        + [listed(2, 64, 16, 1.0), listed(0, 80, 16, 2.0)]
+        + [listed(0, 64, 16, 2.0), listed(2, 80, 16, 1.0), listed(4, 96, 32, 0.0)]
+    )
+    out_hot = jnp.where(match, weight_out * 0.25, 0.0).astype(BF16)
     tot_copy.wait_recv()
-    facts_in = meta_recv[...].reshape(4 * SIDE, W)
-    p_in = (facts_in[:, 0:1].astype(jnp.int32) + C * d) & 255
-    match = lax.broadcasted_iota(jnp.int32, (4 * SIDE, 2 * C), 1) == p_in
-    side_hot = match.astype(F32).astype(BF16)
-    side_total = jnp.sum(jnp.where(match, facts_in[:, 64:65], 0.0), axis=0, keepdims=True)
     totals = own_total[0:1] + tot_recv[0:1, :] + side_total
     inverse = 1.0 / jnp.maximum(totals, 1.0)
 
-    for c in side_arrivals(8, low_rows, side_recv):
+    for c in four_arrivals(9, low_rows, side_recv):
         c.wait_recv()
     from_sides = fold(dot(split(side_recv[...].reshape(4 * SIDE, W).T), side_hot))
     part_copy.wait_recv()
@@ -444,7 +488,7 @@
     group = split(coarse)
     mid = coarse_layer(1, coarse[:, 0:C], group[:, 0:C], lambda: group)
     mid_send[...] = mid
-    mid_copy = copy(13, mid_send, mid_recv, (r, other))
+    mid_copy = copy(14, mid_send, mid_recv, (r, other))
     mid_copy.start()
     mid_split = split(mid)
 
@@ -454,39 +498,66 @@
 
     coarse_out = coarse_layer(2, mid, mid_split, mid_sources)
     co_split = split(coarse_out)
-    reply_send[...] = fold_lanes(dot_nt(side_hot[:, 0:C], co_split)).reshape(4, SIDE, W)
-    replies = side_copies(
-        14,
-        ((reply_send.at[0], reply_send.at[1]), (reply_send.at[2], reply_send.at[3])),
-        reply_recv,
-    )
-    for c in replies:
-        c.start()
     co_send[...] = coarse_out
-    co_copy = copy(18, co_send, co_recv, (r, other))
+    co_copy = copy(15, co_send, co_recv, (r, other))
     co_copy.start()
     cout_ref[...] = coarse_out.T
 
     co_copy.wait_recv()
     known = jnp.concatenate([co_split, split(co_recv[...])], axis=1)
-    added = fold(dot(known, own_hot[...]))
-    for c in side_arrivals(14, reply_send.at[0], reply_recv):
+    given = fold_lanes(dot_nt(out_hot, known))
+    pay_send[...] = given[0:192]
+    pays = [
+        copy(
+            16 + k,
+            pay_send.at[pl.ds(start, size)],
+            pay_recv.at[pl.ds(start, size)],
+            (region, d),
+        )
+        for k, (start, size, region) in enumerate(
+            ((0, 80, up), (80, 80, down), (160, 16, up2), (176, 16, down2))
+        )
+    ]
+    for c in pays:
+        c.start()
+    rows = fine_ref[...] + (share * 0.25) * fold(dot(known, own_hot[...]))
+    fine_own(3, split(rows))
+
+    for c in rims2 + pays:
         c.wait_recv()
-    back = jnp.concatenate(
-        [reply_recv[0] + reply_recv[1], reply_recv[2] + reply_recv[3]], axis=0
+    from_low, from_high = pay_recv[0:32, :], pay_recv[80:112, :]
+    rim = rim2_recv[...] + given[192:256]
+    rim += jnp.concatenate(
+        [
+            pay_recv[64:80, :] + pay_recv[160:176, :],
+            pay_recv[144:160, :] + pay_recv[176:192, :],
+            pay_recv[32:64, :] + pay_recv[112:144, :],
+        ],
+        axis=0,
     )
-    added += fold(dot(split(back.T), side_pick[...]))
-    rows = fine_ref[...] + (share * 0.25) * added
-    rows_split = split(rows)
-    rim2_send[...] = fold_lanes(dot_nt(rim_pick[...], rows_split))
-    rims2 = rim_copies(19, rim2_send, rim2_recv)
-    for c in rims2:
-        c.start()
-    fine_own(3, rows_split)
-    fine_rims(3, rims2, rim2_recv)
-    out_ref[...] = fine_messages(3, rows).T
-
-    for c in rims + metas + [tot_copy] + sides + [part_copy, mid_copy] + replies + [co_copy] + rims2:
+    late = jnp.concatenate([rim, from_low, from_high], axis=0)
+    late_split = split(late.T)
+    side_split = late_split[:, 4 * H :]
+    extra = jnp.concatenate(
+        [split(fold(dot(wts[19], late_split))), split(fold(dot(wts[18], side_split)))], axis=1
+    )
+    rows += fold(dot(side_split, side_pick[...]))
+    node_own[...] += fold(dot(split(fold(dot(wts[21], side_split))), side_pick[...]))
+
+    def late_hot(s, cols):
+        return jnp.concatenate(
+            [
+                one_hot(nbr_ref[pl.ds(s, 1), cols] - F, 4 * H),
+                one_hot(side_ids[pl.ds(s, 1), cols], 2 * SIDE),
+                side_pick[:, cols],
+            ],
+            axis=0,
+        )
+
+    out_ref[...] = fine_messages(3, rows, extra, late_hot).T
+
+    sent = rims + metas + [tot_copy] + sides + [part_copy, mid_copy, co_copy] + pays + rims2
+    for c in sent:
         c.wait_send()
 
 
@@ -505,18 +576,18 @@
             pltpu.VMEM((W, W), F32),
             pltpu.VMEM((24, 2 * W, 2 * W), BF16),
             pltpu.VMEM((SLOTS, W, F), F32),
-            pltpu.VMEM((2 * W, F + 4 * H), BF16),
+            pltpu.VMEM((2 * W + 16, F + 4 * H), BF16),
             pltpu.VMEM((W, F), F32),
             pltpu.VMEM((W, F), F32),
             pltpu.VMEM((W, F), F32),
             pltpu.VMEM((W, F), F32),
-            pltpu.VMEM((4 * H, F), BF16),
-            pltpu.VMEM((2 * SIDE, F), BF16),
+            pltpu.VMEM((2 * SIDE + 4 * H, F), BF16),
             pltpu.VMEM((2 * C, F), BF16),
+            pltpu.VMEM((SLOTS, F), jnp.int32),
             pltpu.VMEM((4 * H, W), F32),
             pltpu.VMEM((4 * H, W), F32),
-            pltpu.VMEM((2 * SIDE, W), F32),
-            pltpu.VMEM((4, SIDE, W), F32),
+            pltpu.VMEM((8, W), F32),
+            pltpu.VMEM((5, 8, W), F32),
             pltpu.VMEM((8, 2 * C), F32),
             pltpu.VMEM((8, 2 * C), F32),
             pltpu.VMEM((W, 2 * C), F32),
@@ -527,12 +598,12 @@
             pltpu.VMEM((W, C), F32),
             pltpu.VMEM((W, C), F32),
             pltpu.VMEM((W, C), F32),
-            pltpu.VMEM((4, SIDE, W), F32),
-            pltpu.VMEM((4, SIDE, W), F32),
+            pltpu.VMEM((192, W), F32),
+            pltpu.VMEM((192, W), F32),
             pltpu.VMEM((4 * H, W), F32),
             pltpu.VMEM((4 * H, W), F32),
-            pltpu.SemaphoreType.DMA((22,)),
-            pltpu.SemaphoreType.DMA((22,)),
+            pltpu.SemaphoreType.DMA((23,)),
+            pltpu.SemaphoreType.DMA((23,)),
             pltpu.SemaphoreType.DMA((13,)),
         ],
         compiler_params=pltpu.CompilerParams(collective_id=0, has_side_effects=True),

time: 52.3 us -> 46.8 us (0.89)
  Pallas kernels: 49.2 us -> 43.7 us
    pallas_call x1, Pallas kernels: 49.2 us -> 43.7 us  [body(): pl.pallas_call(functools.partial(kernel, regions), out_shape=(jax.ShapeDt...]
where the time goes in v2:
time: 46.8 us; the launch traced here: 46.7 us
  Pallas kernels  43.7 us (93%)
  local copies, waits for them, and re-layouts  2.33 us (5%)
  between operations  0.65 us (1%)
    pallas_call x1, Pallas kernels, body(): pl.pallas_call(functools.partial(kernel, regions), out_shape=(jax.ShapeDt...  43.7 us
    unnamed x4, local copies, waits for them, and re-layouts  2.33 us

profile of v2, /device:TPU:1, one launch (start us, length us, event | category | flops | bytes accessed | tf_op | source)
XLA Modules:
  0.0 46.7 jit_solution(427273527624468059)
XLA Ops:
  0.6 43.7 %shard_map.122 = (f32[512,128]{1,0:T(8,128)}, f32[128,128]{1,0:T(8,128)}) custom-call(f32[512,128]{1,0:T(8,128)} %x_in.1, s32[16,512]{1,0:T(8,128)} %nbr_in.1, s32[16,512]{1,0:T(8,128)} %mask_in.1, s32[4,16]{1,0:T(4,128)} %send_in.1, s32[16,128]{1,0:T(8,128)} %cnbr_in.1, s32[16,128]{1,0:T(8,128)} %cmask_in.1, s32[512]{0:T(512)} %parent_in.1, s32[512]{0:T(512)} %share_in.1, ...), custom_call_target="tpu_custom_call" | custom-call | tf_op jit(solution)/shard_map/pallas_call | solution.py:566
  44.3 0.0 copy-start
  44.3 1.7 %copy.15 = f32[512,128]{1,0:T(8,128)} copy(f32[512,128]{1,0:T(8,128)} %get-tuple-element.4) | data formatting | bytes 524288
  46.0 0.0 copy-done
  46.0 0.6 %copy.16 = f32[128,128]{1,0:T(8,128)} copy(f32[128,128]{1,0:T(8,128)S(1)} %copy-done) | data formatting | bytes 131072
Async XLA Ops:
  44.3 1.7 %copy-start = (f32[128,128]{1,0:T(8,128)S(1)}, f32[128,128]{1,0:T(8,128)}, u32[]{:S(2)}) copy-start(f32[128,128]{1,0:T(8,128)} %get-tuple-element.5) | copy-start | bytes 196612

commit v3 on v2

--- a/solution.py
+++ b/solution.py
@@ -316,26 +316,26 @@
         bias1 = jnp.broadcast_to(bias(layer, 1, True), (W, F))
 
         def slots(g, carry):
-            rows4 = [8 * g + k for k in range(8)]
-            for t in range(0, F, 256):
-                cols = pl.ds(t, 256)
+            members = [16 * g + k for k in range(16)]
+            for t in range(0, F, 512):
+                cols = pl.ds(t, 512)
                 total = total_ref[:, cols]
                 hidden = [
-                    base_ref[s, :, cols]
-                    + fold(dot(extra_proj, extra_hot(s, cols)))
-                    for s in rows4
+                    base_ref[s, :, cols] + fold(dot(extra_proj, extra_hot(s, cols)))
+                    for s in members
                 ]
                 hidden = [split(jnp.maximum(h, 0.0)) for h in hidden]
-                centred = [fold(dot(wts[6 * layer + 2], h)) + bias1[:, 0:256] for h in hidden]
+                centred = [fold(dot(wts[6 * layer + 2], h)) + bias1[:, 0:512] for h in hidden]
                 scales = [
-                    scale_of(c) * mask_ref[pl.ds(s, 1), cols].astype(F32) for c, s in zip(centred, rows4)
+                    scale_of(c) * mask_ref[pl.ds(s, 1), cols].astype(F32)
+                    for c, s in zip(centred, members)
                 ]
                 for c, scale in zip(centred, scales):
                     total = total + c * scale
                 total_ref[:, cols] = total
             return carry
 
-        lax.fori_loop(0, SLOTS // 8, slots, 0, unroll=1)
+        lax.fori_loop(0, SLOTS // 16, slots, 0, unroll=1)
         return node_update(
             rows,
             node_own[...],
@@ -416,8 +416,6 @@
     for c in loads[9:]:
         c.wait()
     prepare(1)
-    prepare(2)
-    prepare(3)
     fine_rims(0, rims, rim_recv)
 
     side_share = dot_nt(shares16, side_twice)[0:1]
@@ -444,6 +442,8 @@
     for c in rims2:
         c.start()
 
+    prepare(2)
+
     for c in four_arrivals(3, meta_send, meta_recv) + metas[4:]:
         c.wait_recv()
     tile_ref[0:40, :] = meta_recv[...].reshape(40, W)
@@ -491,6 +491,7 @@
     mid_copy = copy(14, mid_send, mid_recv, (r, other))
     mid_copy.start()
     mid_split = split(mid)
+    prepare(3)
 
     def mid_sources():
         mid_copy.wait_recv()
@@ -561,15 +562,32 @@
         c.wait_send()
 
 
+def hand_over(fine_in, coarse_in, fine_out, coarse_out, fine_tile, coarse_tile, sems):
+    size = F // 4
+    pieces = [(fine_in.at[pl.ds(k * size, size)], fine_tile.at[k], fine_out.at[pl.ds(k * size, size)]) for k in range(4)]
+    pieces.append((coarse_in, coarse_tile, coarse_out))
+    taken = [pltpu.make_async_copy(a, b, sems.at[k]) for k, (a, b, _) in enumerate(pieces)]
+    given = [pltpu.make_async_copy(b, c, sems.at[5 + k]) for k, (_, b, c) in enumerate(pieces)]
+    for c in taken:
+        c.start()
+    for t, g in zip(taken, given):
+        t.wait()
+        g.start()
+    for g in given:
+        g.wait()
+
+
 def body(regions, *args):
     vmem = pl.BlockSpec(memory_space=pltpu.VMEM)
-    return pl.pallas_call(
+    results = (
+        jax.ShapeDtypeStruct((F, W), F32),
+        jax.ShapeDtypeStruct((C, W), F32),
+    )
+    whole = pl.BlockSpec(memory_space=pl.ANY)
+    fine, coarse = pl.pallas_call(
         functools.partial(kernel, regions),
-        out_shape=(
-            jax.ShapeDtypeStruct((F, W), F32),
-            jax.ShapeDtypeStruct((C, W), F32),
-        ),
-        in_specs=[pl.BlockSpec(memory_space=pl.ANY)] * 11,
+        out_shape=results,
+        in_specs=[whole] * 11,
         out_specs=(vmem, vmem),
         scratch_shapes=[pltpu.VMEM(a.shape, a.dtype) for a in args]
         + [
@@ -608,6 +626,17 @@
         ],
         compiler_params=pltpu.CompilerParams(collective_id=0, has_side_effects=True),
     )(*args)
+    return pl.pallas_call(
+        hand_over,
+        out_shape=results,
+        in_specs=[whole] * 2,
+        out_specs=(whole, whole),
+        scratch_shapes=[
+            pltpu.VMEM((4, F // 4, W), F32),
+            pltpu.VMEM((C, W), F32),
+            pltpu.SemaphoreType.DMA((10,)),
+        ],
+    )(fine, coarse)
 
 
 def solution(mesh):

time: 46.8 us -> 45.5 us (0.972)
  local copies, waits for them, and re-layouts: 2.33 us -> 0 us
  Pallas kernels: 43.7 us -> 44.6 us
    unnamed x4 -> x0, local copies, waits for them, and re-layouts: 2.33 us -> none
    pallas_call x1 -> x2, Pallas kernels: 43.7 us -> 44.6 us  [the longest x1 43 us: body(): pl.pallas_call(functools.partial(kernel, regions), out_shape=results, in_...]
where the time goes in v3:
time: 45.5 us; the launch traced here: 45.3 us
  Pallas kernels  44.6 us (98%)
  between operations  0.64 us (1%)
    pallas_call x1, Pallas kernels, body(): pl.pallas_call(functools.partial(kernel, regions), out_shape=results, in_...  43 us
    pallas_call x1, Pallas kernels, body(): pl.pallas_call(hand_over, out_shape=results, in_specs=[whole] * 2, out_sp...  1.68 us

profile of v3, /device:TPU:1, one launch (start us, length us, event | category | flops | bytes accessed | tf_op | source)
XLA Modules:
  0.0 45.3 jit_solution(2362987240629659000)
XLA Ops:
  0.6 43.0 %shard_map.122 = (f32[512,128]{1,0:T(8,128)}, f32[128,128]{1,0:T(8,128)}) custom-call(f32[512,128]{1,0:T(8,128)} %x_in.1, s32[16,512]{1,0:T(8,128)} %nbr_in.1, s32[16,512]{1,0:T(8,128)} %mask_in.1, s32[4,16]{1,0:T(4,128)} %send_in.1, s32[16,128]{1,0:T(8,128)} %cnbr_in.1, s32[16,128]{1,0:T(8,128)} %cmask_in.1, s32[512]{0:T(512)} %parent_in.1, s32[512]{0:T(512)} %share_in.1, ...), custom_call_target="tpu_custom_call" | custom-call | tf_op jit(solution)/shard_map/pallas_call | solution.py:587
  43.6 1.7 %shard_map.123 = (f32[512,128]{1,0:T(8,128)}, f32[128,128]{1,0:T(8,128)}) custom-call(f32[512,128]{1,0:T(8,128)} %get-tuple-element.4.fine_in, f32[128,128]{1,0:T(8,128)} %get-tuple-element.5.coarse_in), custom_call_target="tpu_custom_call" | custom-call | tf_op jit(solution)/shard_map/pallas_call | solution.py:629
